TPU v7x, 256 devices: a whole 4x4x8 slice. The times are simulated.
256 devices in a mesh: strip: 64 (over x, z, core), chan: 4 (over y).
Axes of the slice: x: 4, y: 4, z: 8, core: 2. Of those that a mesh axis runs over, the one named last changes fastest.
Arguments:
- section_input: bfloat16 [48, 8192, 256], P(None, 'strip'), may hold values from -6 to 6
- conv_weight: bfloat16 [3, 3, 256, 256], replicated, may hold values from -0.125 to 0.125
- conv_bias: float32 [256], replicated, may hold values from -3 to 3
- deep_weight: bfloat16 [3, 3, 256, 512], P(None, None, None, 'chan'), may hold values from -0.125 to 0.125
- deep_bias: float32 [512], P('chan'), may hold values from -3 to 3
- labels: int32 [24, 4096], P(None, 'strip'), may hold values from 0 to 32, as said below
- slot_ids: int32 [2048], P('strip'), may hold values from 0 to 4095, as said below
- embed_grad: float32 [4096, 512], P('strip', 'chan'), may hold values from -0.8 to 0.8
Outputs:
- embeddings: float32 [4096, 512], P('strip', 'chan')
- weight_grad: float32 [3, 3, 256, 512], P(None, None, None, 'chan')
- bias_grad: float32 [512], P('chan')
Inputs may be any that keep to these rules, and one draw needn't show every extreme that they name: `labels`: the value 32 marks background; any other value v names entry v of the list of the strip that holds the pixel. `slot_ids`: A value s names slot s % 64 of owner s // 64 (an index of strip). The slots within one strip's list differ; a slot stands in the lists of at most two strips, which are neighbours (a crack across a strip border). Every owner holds at most 64 components and some owner holds exactly 64.
All inputs are finite; a program needn't handle non-finite values.
Results may differ from a plain program's by a relative error of at most 0.0035.
Values may be sent and summed in bfloat16 or wider, within the bound.
A program may use at most 64 MiB of HBM per device.

v0:
```python
import jax
import numpy as np
import jax.numpy as jnp
from jax import lax
from jax.sharding import PartitionSpec as P


def with_halo(cells, sides, width):
    for axis, dim in sides:
        count = lax.axis_size(axis)
        ends = count - 1
        head = lax.slice_in_dim(cells, 0, width, axis=dim)
        tail = lax.slice_in_dim(cells, cells.shape[dim] - width, cells.shape[dim], axis=dim)
        cells = jnp.concatenate(
            [
                lax.ppermute(tail, axis, [(i, (i + 1) % count) for i in range(ends)]),
                cells,
                lax.ppermute(head, axis, [((i + 1) % count, i) for i in range(ends)]),
            ],
            axis=dim,
        )
    return cells


def tree_gather(block, axis, order):
    count = lax.axis_size(axis)
    me = lax.axis_index(axis)
    held = block
    for dist in order:
        other = lax.ppermute(held, axis, [(i, i ^ dist) for i in range(count)])
        high = me // dist % 2
        size = held.shape[0]
        both = jnp.zeros((2 * size,) + held.shape[1:], held.dtype)
        both = lax.dynamic_update_slice_in_dim(both, held, high * size, 0)
        held = lax.dynamic_update_slice_in_dim(both, other, (1 - high) * size, 0)
    return held


def gather_position(order, count):
    return np.array(
        [sum((j // dist % 2 << k for k, dist in enumerate(order))) for j in range(count)], np.int32
    )


def tree_sum(block, axis, rider):
    count = lax.axis_size(axis)
    me = lax.axis_index(axis)
    order = [1 << k for k in range(count.bit_length() - 1)]
    held = block
    for dist in order:
        half = held.shape[0] // 2
        high = me // dist % 2
        keep = lax.dynamic_slice_in_dim(held, high * half, half, 0)
        send = lax.dynamic_slice_in_dim(held, (1 - high) * half, half, 0)
        held = keep + lax.ppermute(send, axis, [(i, i ^ dist) for i in range(count)])
    chunk = held.shape[0]
    both = tree_gather(jnp.concatenate([held, rider], axis=0), axis, order[::-1])
    both = both.reshape(count, chunk + rider.shape[0], *held.shape[1:])
    return (both[:, :chunk].reshape(count * chunk, *held.shape[1:]), both[:, chunk:])


def swish(value):
    return value * jax.nn.sigmoid(value)


def swish_slope(value):
    sigma = jax.nn.sigmoid(value)
    return sigma * (1.0 + value * (1.0 - sigma))


def convolve(padded, weight, row_count, col_count):
    channels = padded.shape[-1]
    running = None
    for shift_row in range(3):
        for shift_col in range(3):
            window = padded[
                shift_row : shift_row + row_count, shift_col : shift_col + col_count
            ].reshape(row_count * col_count, channels)
            partial_term = jnp.dot(
                window, weight[shift_row, shift_col], preferred_element_type=jnp.float32
            )
            running = partial_term if running is None else running + partial_term
    return running.reshape(row_count, col_count, weight.shape[-1])


def pool_pairs(hidden):
    row_count, col_count, channels = hidden.shape
    return (
        hidden.reshape(row_count // 2, 2, col_count // 2, 2, channels)
        .mean(axis=(1, 3))
        .astype(jnp.bfloat16)
    )


def body(
    section_input, conv_weight, conv_bias, deep_weight, deep_bias, labels, slot_ids, embed_grad
):
    chan_count = lax.axis_size("chan")
    chan_pos = lax.axis_index("chan")
    strip_count = lax.axis_size("strip")
    strip_pos = lax.axis_index("strip")
    row_total, col_local, channels = section_input.shape
    row_part = row_total // chan_count
    half_cols = col_local // 2
    list_len = slot_ids.shape[0]
    owned, width_deep = embed_grad.shape
    lanes = embed_grad.shape[1]
    flat_labels = labels.reshape(-1)
    member = flat_labels[None, :] == jnp.arange(list_len, dtype=jnp.int32)[:, None]
    part_counts = jnp.sum(member.astype(jnp.float32), axis=1)
    meta = jnp.zeros((8, lanes), jnp.float32)
    meta = meta.at[0, :list_len].set(part_counts)
    meta = meta.at[0, list_len : 2 * list_len].set(slot_ids.astype(jnp.float32))
    packed = jnp.concatenate([embed_grad, meta], axis=0)
    order = [strip_count >> k + 1 for k in range(strip_count.bit_length() - 1)]
    position = jnp.asarray(gather_position(order, strip_count))
    early = tree_gather(packed, "strip", order[:2])
    padded_rows = jnp.pad(section_input, ((1, 1), (0, 0), (0, 0)))
    own_rows = lax.dynamic_slice_in_dim(padded_rows, chan_pos * row_part, row_part + 2, 0)
    extended = with_halo(own_rows, (("strip", 1),), 3)
    extended, early = lax.optimization_barrier((extended, early))
    early = tree_gather(early, "strip", order[2:4])
    hidden = swish(convolve(extended, conv_weight, row_part, col_local + 4) + conv_bias)
    pooled = pool_pairs(hidden)
    column = jnp.arange(half_cols + 2)
    outside = (column == 0) & (strip_pos == 0) | (column == half_cols + 1) & (
        strip_pos == strip_count - 1
    )
    pooled = jnp.where(outside[None, :, None], jnp.zeros_like(pooled), pooled)
    pooled, early = lax.optimization_barrier((pooled, early))
    every = tree_gather(early, "strip", order[4:]).reshape(strip_count, owned + 8, lanes)
    every_grad = every[:, :owned].reshape(strip_count * owned, lanes)
    every_counts = every[:, owned, :list_len].reshape(-1)
    every_slots = jnp.round(every[:, owned, list_len : 2 * list_len]).astype(jnp.int32).reshape(-1)
    gathered = lax.all_gather(pooled, "chan", axis=0, tiled=True)
    padded_deep = jnp.pad(gathered, ((1, 1), (0, 0), (0, 0)))
    half_rows = gathered.shape[0]
    deep_pre = convolve(padded_deep, deep_weight, half_rows, half_cols) + deep_bias
    features = swish(deep_pre).astype(jnp.bfloat16).reshape(-1, width_deep)
    part_sums = jnp.dot(member.astype(jnp.bfloat16), features, preferred_element_type=jnp.float32)
    same_slot = (slot_ids[:, None] == every_slots[None, :]).astype(jnp.float32)
    entry_counts = jnp.dot(same_slot, every_counts, precision=lax.Precision.HIGHEST)
    grad_row = position[slot_ids // owned] * owned + slot_ids % owned
    entry_grad = every_grad[grad_row] / jnp.maximum(entry_counts, 1.0)[:, None]
    pixel_grad = lax.dot_general(
        member.astype(jnp.float32),
        entry_grad,
        (((0,), (0,)), ((), ())),
        precision=lax.Precision.HIGHEST,
        preferred_element_type=jnp.float32,
    )
    deep_grad = (pixel_grad * swish_slope(deep_pre.reshape(-1, width_deep))).astype(jnp.bfloat16)
    pieces = []
    for shift_row in range(3):
        for shift_col in range(3):
            window = padded_deep[
                shift_row : shift_row + half_rows, shift_col : shift_col + half_cols
            ].reshape(-1, channels)
            pieces.append(
                lax.dot_general(
                    window, deep_grad, (((0,), (0,)), ((), ())), preferred_element_type=jnp.float32
                )
            )
    local_bias = jnp.sum(deep_grad.astype(jnp.float32), axis=0)
    bias_rows = jnp.zeros((strip_count, width_deep), jnp.float32).at[0].set(local_bias)
    local_grads = jnp.concatenate(pieces + [bias_rows], axis=0)
    total_grads, every_sums = tree_sum(local_grads, "strip", part_sums)
    every_sums = every_sums.reshape(-1, width_deep)
    mine = strip_pos * owned + jnp.arange(owned, dtype=jnp.int32)
    pick = (mine[:, None] == every_slots[None, :]).astype(jnp.float32)
    slot_sums = jnp.dot(pick, every_sums, precision=lax.Precision.HIGHEST)
    slot_counts = jnp.dot(pick, every_counts, precision=lax.Precision.HIGHEST)
    embeddings = slot_sums / jnp.maximum(slot_counts, 1.0)[:, None]
    weight_grad = total_grads[: 9 * channels].reshape(3, 3, channels, width_deep)
    bias_grad = total_grads[9 * channels]
    return (embeddings, weight_grad, bias_grad)


def solution(mesh):
    placed = (
        P(None, "strip", None),
        P(),
        P(),
        P(None, None, None, "chan"),
        P("chan"),
        P(None, "strip"),
        P("strip"),
        P("strip", "chan"),
    )
    return jax.shard_map(
        body,
        mesh=mesh,
        in_specs=placed,
        out_specs=(P("strip", "chan"), P(None, None, None, "chan"), P("chan")),
        check_vma=False,
    )
```

profile of v0, /device:TPU:1, one launch (start us, length us, event | category | flops | bytes accessed | tf_op | source)
XLA Modules:
  0.0 212.5 jit_solution(15142694964070461759)
XLA Ops:
  0.7 0.8 eq.95
  2.2 1.3 and_reduce_fusion
  3.5 2.7 %broadcast_select_fusion = f32[1,32]{1,0:T(1,128)S(1)} fusion(pred[]{:T(512)} %and_reduce_fusion, s32[]{:T(128)} %bitcast.2, s32[]{:T(128)} %bitcast.3, f32[1,32]{1,0:T(1,128)S(1)} %bitcast.147, s32[32]{0:T(128)} %param.21), kind=kLoop, calls=%fused_computation.155 | loop fusion | flops 64 | bytes 393 | tf_op jit(solution)/shard_map/select.4
  6.2 1.6 scatter.11
  7.7 0.8 pad_maximum_fusion.1
  8.5 3.6 %collective-permute-start.2 = (f32[72,128]{1,0:T(8,128)S(1)}, f32[72,128]{1,0:T(8,128)S(1)}, u32[]{:S(2)}, u32[]{:S(2)}) collective-permute-start(f32[72,128]{1,0:T(8,128)S(1)} %get-tuple-element.67), channel_id=1, source_target_pairs={{0,128},{4,132},{8,136},{12,140},{16,144},{20,148},{24,152},{28,15... | collective-permute-start | bytes 110600 | tf_op jit(solution)/shard_map/ppermute | solution.py:30
  12.1 1.0 pad_dynamic-slice_fusion.1
  13.1 4.4 %collective-permute-start = (bf16[14,3,256]{2,1,0:T(4,128)(2,1)S(1)}, bf16[14,3,256]{2,1,0:T(4,128)(2,1)S(1)}, u32[]{:S(2)}, u32[]{:S(2)}) collective-permute-start(bf16[14,3,256]{2,1,0:T(4,128)(2,1)S(1)} %get-tuple-element.47), channel_id=1, source_target_pairs={{0,4},{4,8},{8,12},{12,16},{16,20},{20,24},{24,28},{28,32},{32,36}... | collective-permute-start | bytes 64520 | tf_op jit(solution)/shard_map/ppermute | solution.py:16
  17.5 1.9 collective-permute-start.1
  20.6 2.2 %collective-permute-done.1 = bf16[14,3,256]{2,1,0:T(4,128)(2,1)S(1)} collective-permute-done((bf16[14,3,256]{2,1,0:T(4,128)(2,1)S(1)}, bf16[14,3,256]{2,1,0:T(4,128)(2,1)S(1)}, u32[]{:S(2)}, u32[]{:S(2)}) %collective-permute-start.1) | collective-permute-done | bytes 21536 | tf_op jit(solution)/shard_map/ppermute | solution.py:18
  23.9 2.6 %collective-permute-done.3 = f32[144,128]{1,0:T(8,128)S(1)} collective-permute-done((f32[144,128]{1,0:T(8,128)S(1)}, f32[144,128]{1,0:T(8,128)S(1)}, u32[]{:S(2)}, u32[]{:S(2)}) %collective-permute-start.3) | collective-permute-done | bytes 73760 | tf_op jit(solution)/shard_map/ppermute | solution.py:30
  26.5 6.3 %collective-permute-start.4 = (f32[288,128]{1,0:T(8,128)S(1)}, f32[288,128]{1,0:T(8,128)}, u32[]{:S(2)}, u32[]{:S(2)}) collective-permute-start(f32[288,128]{1,0:T(8,128)S(1)} %constant_dynamic-update-slice_fusion.14), channel_id=1, source_target_pairs={{0,32},{4,36},{8,40},{12,44},{16,48},{20,52},{24,56},{28,60},{32,0... | collective-permute-start | bytes 442376 | tf_op jit(solution)/shard_map/ppermute | solution.py:30
  32.8 2.5 %fusion.62 = (bf16[12,132,256]{2,1,0:T(8,128)(2,1)S(1)}, bf16[12,132,256]{2,1,0:T(8,128)(2,1)S(1)}, bf16[12,132,256]{2,1,0:T(8,128)(2,1)S(1)}, bf16[12,132,256]{...) fusion(bf16[14,134,256]{2,1,0:T(8,128)(2,1)S(1)} %pad_maximum_f, ...), kind=kLoop, calls=%fused_computation.161 | loop fusion | bytes 14598144 | tf_op jit(solution)/shard_map/slice | solution.py:76
  35.3 2.0 reshape.215
  37.3 2.1 reshape.216
  39.4 2.0 reshape.217
  41.4 2.1 reshape.218
  43.5 2.0 reshape.219
  45.5 1.0 reshape.220
  46.6 1.0 reshape.221
  47.8 1.1 reshape.223
  48.8 1.4 fusion.22
  51.9 0.8 copy-done.17
  54.2 0.8 copy-done.15
  58.0 1.0 reshape.224
  59.0 2.7 %fusion.2 = f32[6,66,256]{2,1,0:T(8,128)S(1)} fusion(f32[6,2,66,2,256]{4,3,2,1,0:T(2,128)S(1)} %reshape.224, f32[256]{0:T(256)S(1)} %copy-done.24), kind=kLoop, calls=%fused_computation.25 | loop fusion | flops 2331648 | bytes 2028544 | tf_op jit(solution)/shard_map/reduce_sum | solution.py:90
  61.8 0.9 constant_dynamic-update-slice_fusion.12
  62.7 2.1 collective-permute-start.5
  64.9 12.7 %collective-permute-done.5 = f32[576,128]{1,0:T(8,128)S(1)} collective-permute-done((f32[576,128]{1,0:T(8,128)S(1)}, f32[576,128]{1,0:T(8,128)S(1)}, u32[]{:S(2)}, u32[]{:S(2)}) %collective-permute-start.5) | collective-permute-done | bytes 294944 | tf_op jit(solution)/shard_map/ppermute | solution.py:30
  78.0 12.9 %all_gather.3 = bf16[24,66,256]{2,1,0:T(8,128)(2,1)S(1)} all-gather(bf16[6,66,256]{2,1,0:T(8,128)(2,1)S(1)} %fusion.13), channel_id=1, replica_groups=mesh['strip'=64,'chan'=4] {'chan'}, dimensions={0}, use_global_device_ids=true | all-gather | bytes 1013760 | tf_op jit(solution)/shard_map/all_gather | solution.py:135
  90.8 1.4 pad_slice_fusion
  95.4 3.7 %collective-permute-start.7 = (f32[2304,128]{1,0:T(8,128)S(1)}, f32[2304,128]{1,0:T(8,128)S(1)}, u32[]{:S(2)}, u32[]{:S(2)}) collective-permute-start(f32[2304,128]{1,0:T(8,128)S(1)} %constant_dynamic-update-slice_fusion.8), channel_id=1, source_target_pairs={{0,4},{4,0},{8,12},{12,8},{16,20},{20,16},{24,28},{28,24},{32,36},... | collective-permute-start | bytes 3538952 | tf_op jit(solution)/shard_map/ppermute | solution.py:30
  100.1 1.3 fusion
  102.0 1.6 slice.251
  104.0 2.2 %gather_fusion.1 = f32[32,128]{1,0:T(8,128)S(1)} fusion(f32[4096,128]{1,0:T(8,128)} %bitcast.144, s32[1024]{0:T(1024)S(1)} %pad_clamp_fusion), kind=kCustom, calls=%fused_computation.1 | custom fusion | bytes 32896 | tf_op jit(solution)/shard_map/gather | solution.py:144
  106.2 2.1 convert_reduce_fusion
  113.1 1.0 copy-done.20
  114.6 1.7 collective-permute-done.8
  116.3 1.1 dynamic-slice_add_fusion
  117.5 1.8 collective-permute-start.9
  119.3 7.3 %collective-permute-done.9 = f32[592,128]{1,0:T(8,128)S(1)} collective-permute-done((f32[592,128]{1,0:T(8,128)S(1)}, f32[592,128]{1,0:T(8,128)S(1)}, u32[]{:S(2)}, u32[]{:S(2)}) %collective-permute-start.9) | collective-permute-done | bytes 303136 | tf_op jit(solution)/shard_map/ppermute | solution.py:55
  126.6 2.2 %collective-permute-start.10 = (f32[296,128]{1,0:T(8,128)S(1)}, f32[296,128]{1,0:T(8,128)S(1)}, u32[]{:S(2)}, u32[]{:S(2)}) collective-permute-start(f32[296,128]{1,0:T(8,128)S(1)} %constant_dynamic-slice_fusion.3), channel_id=1, source_target_pairs={{0,16},{4,20},{8,24},{12,28},{16,0},{20,4},{24,8},{28,12},{32,48},... | collective-permute-start | bytes 454664 | tf_op jit(solution)/shard_map/ppermute | solution.py:55
  128.8 6.9 %collective-permute-done.10 = f32[296,128]{1,0:T(8,128)S(1)} collective-permute-done((f32[296,128]{1,0:T(8,128)S(1)}, f32[296,128]{1,0:T(8,128)S(1)}, u32[]{:S(2)}, u32[]{:S(2)}) %collective-permute-start.10) | collective-permute-done | bytes 151584 | tf_op jit(solution)/shard_map/ppermute | solution.py:55
  136.2 6.8 %collective-permute-done.11 = f32[148,128]{1,0:T(8,128)S(1)} collective-permute-done((f32[148,128]{1,0:T(8,128)S(1)}, f32[148,128]{1,0:T(8,128)S(1)}, u32[]{:S(2)}, u32[]{:S(2)}) %collective-permute-start.11) | collective-permute-done | bytes 75808 | tf_op jit(solution)/shard_map/ppermute | solution.py:55
  143.4 2.5 %collective-permute-done.12 = f32[74,128]{1,0:T(8,128)S(1)} collective-permute-done((f32[74,128]{1,0:T(8,128)S(1)}, f32[74,128]{1,0:T(8,128)S(1)}, u32[]{:S(2)}, u32[]{:S(2)}) %collective-permute-start.12) | collective-permute-done | bytes 37920 | tf_op jit(solution)/shard_map/ppermute | solution.py:55
  146.0 1.2 collective-permute-start.13
  147.5 3.0 %collective-permute-done.13 = f32[37,128]{1,0:T(8,128)S(1)} collective-permute-done((f32[37,128]{1,0:T(8,128)S(1)}, f32[37,128]{1,0:T(8,128)S(1)}, u32[]{:S(2)}, u32[]{:S(2)}) %collective-permute-start.13) | collective-permute-done | bytes 18976 | tf_op jit(solution)/shard_map/ppermute | solution.py:55
  150.5 0.9 collective-permute-start.14
  151.8 3.6 %collective-permute-done.14 = f32[69,128]{1,0:T(8,128)S(1)} collective-permute-done((f32[69,128]{1,0:T(8,128)S(1)}, f32[69,128]{1,0:T(8,128)S(1)}, u32[]{:S(2)}, u32[]{:S(2)}) %collective-permute-start.14) | collective-permute-done | bytes 35360 | tf_op jit(solution)/shard_map/ppermute | solution.py:30
  156.4 2.9 %collective-permute-done.15 = f32[138,128]{1,0:T(8,128)S(1)} collective-permute-done((f32[138,128]{1,0:T(8,128)S(1)}, f32[138,128]{1,0:T(8,128)S(1)}, u32[]{:S(2)}, u32[]{:S(2)}) %collective-permute-start.15) | collective-permute-done | bytes 70688 | tf_op jit(solution)/shard_map/ppermute | solution.py:30
  159.8 1.1 dynamic_update_slice.88
  160.9 6.7 %collective-permute-done.16 = f32[276,128]{1,0:T(8,128)S(1)} collective-permute-done((f32[276,128]{1,0:T(8,128)S(1)}, f32[276,128]{1,0:T(8,128)S(1)}, u32[]{:S(2)}, u32[]{:S(2)}) %collective-permute-start.16) | collective-permute-done | bytes 141344 | tf_op jit(solution)/shard_map/ppermute | solution.py:30
  168.5 11.4 %collective-permute-done.17 = f32[552,128]{1,0:T(8,128)S(1)} collective-permute-done((f32[552,128]{1,0:T(8,128)S(1)}, f32[552,128]{1,0:T(8,128)S(1)}, u32[]{:S(2)}, u32[]{:S(2)}) %collective-permute-start.17) | collective-permute-done | bytes 282656 | tf_op jit(solution)/shard_map/ppermute | solution.py:30
  180.1 12.5 %collective-permute-done.18 = f32[1104,128]{1,0:T(8,128)S(1)} collective-permute-done((f32[1104,128]{1,0:T(8,128)S(1)}, f32[1104,128]{1,0:T(8,128)S(1)}, u32[]{:S(2)}, u32[]{:S(2)}) %collective-permute-start.18) | collective-permute-done | bytes 565280 | tf_op jit(solution)/shard_map/ppermute | solution.py:30
  192.7 5.6 %collective-permute-start.19 = (f32[2208,128]{1,0:T(8,128)S(1)}, f32[2208,128]{1,0:T(8,128)S(1)}, u32[]{:S(2)}, u32[]{:S(2)}) collective-permute-start(f32[2208,128]{1,0:T(8,128)S(1)} %constant_dynamic-update-slice_fusion.2), channel_id=1, source_target_pairs={{0,4},{4,0},{8,12},{12,8},{16,20},{20,16},{24,28},{28,24},{32,36},... | collective-permute-start | bytes 3391496 | tf_op jit(solution)/shard_map/ppermute | solution.py:30
  198.6 1.6 broadcast_in_dim.71
  200.2 1.1 constant_dynamic-update-slice_fusion.1
  201.3 1.1 constant_dynamic-update-slice_fusion
  202.4 1.7 reshape.237
  204.1 1.2 slice.257
  205.2 2.4 %reshape.239 = f32[2368,128]{1,0:T(8,128)} reshape(f32[64,37,128]{2,1,0:T(8,128)} %slice.257) | data formatting | bytes 2424832 | tf_op jit(solution)/shard_map/reshape | solution.py:59
  207.6 2.4 %slice.258 = f32[2304,128]{1,0:T(8,128)} slice(f32[2368,128]{1,0:T(8,128)} %reshape.239), slice={[0:2304], [0:128]} | slice | bytes 2359296 | tf_op jit(solution)/shard_map/slice | solution.py:174
  210.0 1.2 slice_bitcast_fusion
  211.3 1.2 convolution_divide_fusion
  (157 shorter events, 24.7 us)
Async XLA Ops:
  8.5 14.6 %collective-permute-start.2 = (f32[72,128]{1,0:T(8,128)S(1)}, f32[72,128]{1,0:T(8,128)S(1)}, u32[]{:S(2)}, u32[]{:S(2)}) collective-permute-start(f32[72,128]{1,0:T(8,128)S(1)} %get-tuple-element.67), channel_id=1, source_target_pairs={{0,128},{4,132},{8,136},{12,140},{16,144},{20,148},{24,152},{28,15... | collective-permute-start | bytes 110600 | tf_op jit(solution)/shard_map/ppermute | solution.py:30
  12.1 7.4 %copy-start.1 = (bf16[48,128,256]{2,1,0:T(8,128)(2,1)S(1)}, bf16[48,128,256]{2,1,0:T(8,128)(2,1)}, u32[]{:S(2)}) copy-start(bf16[48,128,256]{2,1,0:T(8,128)(2,1)} %param.15) | copy-start | bytes 9437188
  13.1 7.4 %collective-permute-start = (bf16[14,3,256]{2,1,0:T(4,128)(2,1)S(1)}, bf16[14,3,256]{2,1,0:T(4,128)(2,1)S(1)}, u32[]{:S(2)}, u32[]{:S(2)}) collective-permute-start(bf16[14,3,256]{2,1,0:T(4,128)(2,1)S(1)} %get-tuple-element.47), channel_id=1, source_target_pairs={{0,4},{4,8},{8,12},{12,16},{16,20},{20,24},{24,28},{28,32},{32,36}... | collective-permute-start | bytes 64520 | tf_op jit(solution)/shard_map/ppermute | solution.py:16
  17.5 2.1 copy-start.25
  17.5 2.1 copy-start
  17.5 5.2 %collective-permute-start.1 = (bf16[14,3,256]{2,1,0:T(4,128)(2,1)S(1)}, bf16[14,3,256]{2,1,0:T(4,128)(2,1)S(1)}, u32[]{:S(2)}, u32[]{:S(2)}) collective-permute-start(bf16[14,3,256]{2,1,0:T(4,128)(2,1)S(1)} %get-tuple-element.48), channel_id=1, source_target_pairs={{4,0},{8,4},{12,8},{16,12},{20,16},{24,20},{28,24},{32,28},{36,32}... | collective-permute-start | bytes 64520 | tf_op jit(solution)/shard_map/ppermute | solution.py:18
  23.2 3.3 %collective-permute-start.3 = (f32[144,128]{1,0:T(8,128)S(1)}, f32[144,128]{1,0:T(8,128)S(1)}, u32[]{:S(2)}, u32[]{:S(2)}) collective-permute-start(f32[144,128]{1,0:T(8,128)S(1)} %constant_dynamic-update-slice_fusion.16), channel_id=1, source_target_pairs={{0,64},{4,68},{8,72},{12,76},{16,80},{20,84},{24,88},{28,92},{32,9... | collective-permute-start | bytes 221192 | tf_op jit(solution)/shard_map/ppermute | solution.py:30
  26.5 35.3 %collective-permute-start.4 = (f32[288,128]{1,0:T(8,128)S(1)}, f32[288,128]{1,0:T(8,128)}, u32[]{:S(2)}, u32[]{:S(2)}) collective-permute-start(f32[288,128]{1,0:T(8,128)S(1)} %constant_dynamic-update-slice_fusion.14), channel_id=1, source_target_pairs={{0,32},{4,36},{8,40},{12,44},{16,48},{20,52},{24,56},{28,60},{32,0... | collective-permute-start | bytes 442376 | tf_op jit(solution)/shard_map/ppermute | solution.py:30
  47.6 1.2 copy-start.12
  48.8 1.4 copy-start.19
  48.8 1.6 copy-start.21
  50.4 1.1 copy-start.18
  51.5 1.1 copy-start.17
  52.7 1.1 copy-start.16
  53.8 1.1 copy-start.15
  55.0 1.1 copy-start.14
  56.5 1.1 copy-start.13
  58.0 1.0 copy-start.24
  62.7 14.9 %collective-permute-start.5 = (f32[576,128]{1,0:T(8,128)S(1)}, f32[576,128]{1,0:T(8,128)S(1)}, u32[]{:S(2)}, u32[]{:S(2)}) collective-permute-start(f32[576,128]{1,0:T(8,128)S(1)} %constant_dynamic-update-slice_fusion.12), channel_id=1, source_target_pairs={{0,16},{4,20},{8,24},{12,28},{16,0},{20,4},{24,8},{28,12},{32,48},... | collective-permute-start | bytes 884744 | tf_op jit(solution)/shard_map/ppermute | solution.py:30
  77.7 17.6 %collective-permute-start.6 = (f32[1152,128]{1,0:T(8,128)S(1)}, f32[1152,128]{1,0:T(8,128)S(1)}, u32[]{:S(2)}, u32[]{:S(2)}) collective-permute-start(f32[1152,128]{1,0:T(8,128)S(1)} %constant_dynamic-update-slice_fusion.10), channel_id=1, source_target_pairs={{0,8},{4,12},{8,0},{12,4},{16,24},{20,28},{24,16},{28,20},{32,40},... | collective-permute-start | bytes 1769480 | tf_op jit(solution)/shard_map/ppermute | solution.py:30
  90.8 1.4 copy-start.23
  92.2 0.9 copy-start.8
  92.2 1.2 copy-start.10
  92.3 1.4 copy-start.6
  92.3 1.8 copy-start.4
  92.3 2.3 %copy-start.2 = (bf16[24,64,256]{2,1,0:T(8,128)(2,1)}, bf16[24,64,256]{2,1,0:T(8,128)(2,1)S(1)}, u32[]{:S(2)}) copy-start(bf16[24,64,256]{2,1,0:T(8,128)(2,1)S(1)} %get-tuple-element.64) | copy-start | bytes 2359300
  95.4 6.2 %collective-permute-start.7 = (f32[2304,128]{1,0:T(8,128)S(1)}, f32[2304,128]{1,0:T(8,128)S(1)}, u32[]{:S(2)}, u32[]{:S(2)}) collective-permute-start(f32[2304,128]{1,0:T(8,128)S(1)} %constant_dynamic-update-slice_fusion.8), channel_id=1, source_target_pairs={{0,4},{4,0},{8,12},{12,8},{16,20},{20,16},{24,28},{28,24},{32,36},... | collective-permute-start | bytes 3538952 | tf_op jit(solution)/shard_map/ppermute | solution.py:30
  99.4 0.7 copy-start.26
  106.2 2.1 copy-start.11
  108.3 1.1 copy-start.9
  108.3 1.5 copy-start.7
  109.4 1.2 copy-start.5
  109.8 1.2 copy-start.3
  113.1 1.0 copy-start.20
  114.2 2.1 collective-permute-start.8
  117.5 29.7 %copy-start.22 = (f32[1536,128]{1,0:T(8,128)S(1)}, f32[1536,128]{1,0:T(8,128)}, u32[]{:S(2)}) copy-start(f32[1536,128]{1,0:T(8,128)} %fusion) | copy-start | bytes 2359300
  117.5 9.0 %collective-permute-start.9 = (f32[592,128]{1,0:T(8,128)S(1)}, f32[592,128]{1,0:T(8,128)S(1)}, u32[]{:S(2)}, u32[]{:S(2)}) collective-permute-start(f32[592,128]{1,0:T(8,128)S(1)} %constant_dynamic-slice_fusion.4), channel_id=1, source_target_pairs={{0,8},{4,12},{8,0},{12,4},{16,24},{20,28},{24,16},{28,20},{32,40},... | collective-permute-start | bytes 909320 | tf_op jit(solution)/shard_map/ppermute | solution.py:55
  126.6 9.1 %collective-permute-start.10 = (f32[296,128]{1,0:T(8,128)S(1)}, f32[296,128]{1,0:T(8,128)S(1)}, u32[]{:S(2)}, u32[]{:S(2)}) collective-permute-start(f32[296,128]{1,0:T(8,128)S(1)} %constant_dynamic-slice_fusion.3), channel_id=1, source_target_pairs={{0,16},{4,20},{8,24},{12,28},{16,0},{20,4},{24,8},{28,12},{32,48},... | collective-permute-start | bytes 454664 | tf_op jit(solution)/shard_map/ppermute | solution.py:55
  135.8 7.2 %collective-permute-start.11 = (f32[148,128]{1,0:T(8,128)S(1)}, f32[148,128]{1,0:T(8,128)S(1)}, u32[]{:S(2)}, u32[]{:S(2)}) collective-permute-start(f32[148,128]{1,0:T(8,128)S(1)} %constant_dynamic-slice_fusion.2), channel_id=1, source_target_pairs={{0,32},{4,36},{8,40},{12,44},{16,48},{20,52},{24,56},{28,60},{32,0... | collective-permute-start | bytes 227336 | tf_op jit(solution)/shard_map/ppermute | solution.py:55
  143.0 2.9 %collective-permute-start.12 = (f32[74,128]{1,0:T(8,128)S(1)}, f32[74,128]{1,0:T(8,128)S(1)}, u32[]{:S(2)}, u32[]{:S(2)}) collective-permute-start(f32[74,128]{1,0:T(8,128)S(1)} %constant_dynamic-slice_fusion.1), channel_id=1, source_target_pairs={{0,64},{4,68},{8,72},{12,76},{16,80},{20,84},{24,88},{28,92},{32,9... | collective-permute-start | bytes 113672 | tf_op jit(solution)/shard_map/ppermute | solution.py:55
  146.0 4.5 %collective-permute-start.13 = (f32[37,128]{1,0:T(8,128)S(1)}, f32[37,128]{1,0:T(8,128)S(1)}, u32[]{:S(2)}, u32[]{:S(2)}) collective-permute-start(f32[37,128]{1,0:T(8,128)S(1)} %constant_dynamic-slice_fusion), channel_id=1, source_target_pairs={{0,128},{4,132},{8,136},{12,140},{16,144},{20,148},{24,152},{28,15... | collective-permute-start | bytes 56840 | tf_op jit(solution)/shard_map/ppermute | solution.py:55
  150.5 4.9 %collective-permute-start.14 = (f32[69,128]{1,0:T(8,128)S(1)}, f32[69,128]{1,0:T(8,128)S(1)}, u32[]{:S(2)}, u32[]{:S(2)}) collective-permute-start(f32[69,128]{1,0:T(8,128)S(1)} %pad_maximum_fusion.2), channel_id=1, source_target_pairs={{0,128},{4,132},{8,136},{12,140},{16,144},{20,148},{24,152},{28,15... | collective-permute-start | bytes 105992 | tf_op jit(solution)/shard_map/ppermute | solution.py:30
  155.6 3.7 %collective-permute-start.15 = (f32[138,128]{1,0:T(8,128)S(1)}, f32[138,128]{1,0:T(8,128)S(1)}, u32[]{:S(2)}, u32[]{:S(2)}) collective-permute-start(f32[138,128]{1,0:T(8,128)S(1)} %dynamic_update_slice.85), channel_id=1, source_target_pairs={{0,64},{4,68},{8,72},{12,76},{16,80},{20,84},{24,88},{28,92},{32,9... | collective-permute-start | bytes 211976 | tf_op jit(solution)/shard_map/ppermute | solution.py:30
  159.7 7.9 %collective-permute-start.16 = (f32[276,128]{1,0:T(8,128)S(1)}, f32[276,128]{1,0:T(8,128)S(1)}, u32[]{:S(2)}, u32[]{:S(2)}) collective-permute-start(f32[276,128]{1,0:T(8,128)S(1)} %dynamic_update_slice.87), channel_id=1, source_target_pairs={{0,32},{4,36},{8,40},{12,44},{16,48},{20,52},{24,56},{28,60},{32,0... | collective-permute-start | bytes 423944 | tf_op jit(solution)/shard_map/ppermute | solution.py:30
  168.3 11.6 %collective-permute-start.17 = (f32[552,128]{1,0:T(8,128)S(1)}, f32[552,128]{1,0:T(8,128)S(1)}, u32[]{:S(2)}, u32[]{:S(2)}) collective-permute-start(f32[552,128]{1,0:T(8,128)S(1)} %dynamic_update_slice.89), channel_id=1, source_target_pairs={{0,16},{4,20},{8,24},{12,28},{16,0},{20,4},{24,8},{28,12},{32,48},... | collective-permute-start | bytes 847880 | tf_op jit(solution)/shard_map/ppermute | solution.py:30
  179.9 12.8 %collective-permute-start.18 = (f32[1104,128]{1,0:T(8,128)S(1)}, f32[1104,128]{1,0:T(8,128)S(1)}, u32[]{:S(2)}, u32[]{:S(2)}) collective-permute-start(f32[1104,128]{1,0:T(8,128)S(1)} %constant_dynamic-update-slice_fusion.4), channel_id=1, source_target_pairs={{0,8},{4,12},{8,0},{12,4},{16,24},{20,28},{24,16},{28,20},{32,40},... | collective-permute-start | bytes 1695752 | tf_op jit(solution)/shard_map/ppermute | solution.py:30
  192.7 8.6 %collective-permute-start.19 = (f32[2208,128]{1,0:T(8,128)S(1)}, f32[2208,128]{1,0:T(8,128)S(1)}, u32[]{:S(2)}, u32[]{:S(2)}) collective-permute-start(f32[2208,128]{1,0:T(8,128)S(1)} %constant_dynamic-update-slice_fusion.2), channel_id=1, source_target_pairs={{0,4},{4,0},{8,12},{12,8},{16,20},{20,16},{24,28},{28,24},{32,36},... | collective-permute-start | bytes 3391496 | tf_op jit(solution)/shard_map/ppermute | solution.py:30
where the time goes:
time: 213 us; the launch traced here: 212 us
  waiting for transfers between devices  82.6 us (39%)
  local copies, waits for them, and re-layouts  53 us (25%)
  starting transfers between devices  36.2 us (17%)
  matrix products  16.5 us (8%)
  blocking collectives  12.9 us (6%)
  other arithmetic  9.54 us (4%)
    ppermute x12, waiting for transfers between devices, tree_gather(): other = lax.ppermute(held, axis, [(i, i ^ dist) for i in range(count)])  52.3 us
    ppermute x6, waiting for transfers between devices, tree_sum(): lax.ppermute(send, axis, [(i, i ^ dist) for i in range(count)])  28.2 us
    ppermute x12, starting transfers between devices, tree_gather(): other = lax.ppermute(held, axis, [(i, i ^ dist) for i in range(count)])  23.5 us
    reshape x9, local copies, waits for them, and re-layouts, convolve(): window = padded[shift_row:shift_row + row_count, shift_col:shift_col + co...  13.5 us
    all_gather x1, blocking collectives, body(): gathered = lax.all_gather(pooled, 'chan', axis=0, tiled=True)  12.9 us
    dot_general x18, matrix products, convolve(): jnp.dot(window, weight[shift_row, shift_col], preferred_element_type=jnp....  8.6 us
    unnamed x54, local copies, waits for them, and re-layouts  7.77 us
    ppermute x6, starting transfers between devices, tree_sum(): lax.ppermute(send, axis, [(i, i ^ dist) for i in range(count)])  6.37 us
  transfers between devices with their start and end apart: 20, of which 14 were waited for; matrix products, arithmetic and copies ran while one was open for 18% of the time, Pallas kernels for 0%

commit v1 on v0

--- a/solution.py
+++ b/solution.py
@@ -132,7 +132,9 @@
     every_grad = every[:, :owned].reshape(strip_count * owned, lanes)
     every_counts = every[:, owned, :list_len].reshape(-1)
     every_slots = jnp.round(every[:, owned, list_len : 2 * list_len]).astype(jnp.int32).reshape(-1)
-    gathered = lax.all_gather(pooled, "chan", axis=0, tiled=True)
+    gathered = jnp.concatenate(
+        lax.all_to_all(jnp.stack([pooled] * lax.axis_size("chan")), "chan", 0, 0), axis=0
+    )
     padded_deep = jnp.pad(gathered, ((1, 1), (0, 0), (0, 0)))
     half_rows = gathered.shape[0]
     deep_pre = convolve(padded_deep, deep_weight, half_rows, half_cols) + deep_bias

time: 213 us -> 216 us (1.014)
  blocking collectives: 12.9 us -> 0 us
  starting transfers between devices: 36.2 us -> 44.2 us
  local copies, waits for them, and re-layouts: 53 us -> 59.1 us
  waiting for transfers between devices: 82.6 us -> 86.2 us
  matrix products: 16.5 us -> 14.3 us
    all_gather x1 -> x0, blocking collectives: 12.9 us -> none  [body(): gathered = lax.all_gather(pooled, 'chan', axis=0, tiled=True)]
    all_to_all x0 -> x1, starting transfers between devices: none -> 4.17 us  [body(): lax.all_to_all(jnp.stack([pooled] * lax.axis_size('chan')), 'chan', 0, 0)]
    ppermute x6, starting transfers between devices: 6.37 us -> 9.42 us  [tree_sum(): lax.ppermute(send, axis, [(i, i ^ dist) for i in range(count)])]
    ppermute x12, waiting for transfers between devices: 52.3 us -> 54.5 us  [tree_gather(): other = lax.ppermute(held, axis, [(i, i ^ dist) for i in range(count)])]
    unnamed x54 -> x66, local copies, waits for them, and re-layouts: 7.77 us -> 7.39 us
  transfers between devices with their start and end apart: 20 -> 21, of which waited for: 14 -> 15; matrix products, arithmetic and copies ran while one was open for 18% -> 20% of each run, Pallas kernels for 0% -> 0%
where the time goes in v1:
time: 216 us; the launch traced here: 215 us
  waiting for transfers between devices  86.2 us (40%)
  local copies, waits for them, and re-layouts  59.1 us (27%)
  starting transfers between devices  44.2 us (20%)
  matrix products  14.3 us (7%)
  other arithmetic  9.54 us (4%)
    ppermute x12, waiting for transfers between devices, tree_gather(): other = lax.ppermute(held, axis, [(i, i ^ dist) for i in range(count)])  54.5 us
    ppermute x6, waiting for transfers between devices, tree_sum(): lax.ppermute(send, axis, [(i, i ^ dist) for i in range(count)])  28.8 us
    ppermute x12, starting transfers between devices, tree_gather(): other = lax.ppermute(held, axis, [(i, i ^ dist) for i in range(count)])  24.3 us
    reshape x9, local copies, waits for them, and re-layouts, convolve(): window = padded[shift_row:shift_row + row_count, shift_col:shift_col + co...  13.6 us
    ppermute x6, starting transfers between devices, tree_sum(): lax.ppermute(send, axis, [(i, i ^ dist) for i in range(count)])  9.42 us
    dot_general x18, matrix products, convolve(): jnp.dot(window, weight[shift_row, shift_col], preferred_element_type=jnp....  7.7 us
    unnamed x66, local copies, waits for them, and re-layouts  7.39 us
    dynamic_update_slice x12, local copies, waits for them, and re-layouts, tree_gather(): held = lax.dynamic_update_slice_in_dim(both, other, (1 - high) * size, 0)  5.57 us
  transfers between devices with their start and end apart: 21, of which 15 were waited for; matrix products, arithmetic and copies ran while one was open for 20% of the time, Pallas kernels for 0%

profile of v1, /device:TPU:1, one launch (start us, length us, event | category | flops | bytes accessed | tf_op | source)
XLA Modules:
  0.0 215.2 jit_solution(2696807104057699736)
XLA Ops:
  2.2 1.3 and_reduce_fusion
  3.5 2.7 %broadcast_select_fusion = f32[1,32]{1,0:T(1,128)S(1)} fusion(pred[]{:T(512)} %and_reduce_fusion, s32[]{:T(128)} %bitcast.2, s32[]{:T(128)} %bitcast.3, f32[1,32]{1,0:T(1,128)S(1)} %bitcast.149, s32[32]{0:T(128)} %param.21), kind=kLoop, calls=%fused_computation.155 | loop fusion | flops 64 | bytes 393 | tf_op jit(solution)/shard_map/select.4
  6.2 1.6 scatter.11
  8.5 3.6 %collective-permute-start.2 = (f32[72,128]{1,0:T(8,128)S(1)}, f32[72,128]{1,0:T(8,128)S(1)}, u32[]{:S(2)}, u32[]{:S(2)}) collective-permute-start(f32[72,128]{1,0:T(8,128)S(1)} %get-tuple-element.67), channel_id=1, source_target_pairs={{0,128},{4,132},{8,136},{12,140},{16,144},{20,148},{24,152},{28,15... | collective-permute-start | bytes 110600 | tf_op jit(solution)/shard_map/ppermute | solution.py:30
  12.1 1.0 pad_dynamic-slice_fusion.1
  13.1 4.4 %collective-permute-start = (bf16[14,3,256]{2,1,0:T(4,128)(2,1)S(1)}, bf16[14,3,256]{2,1,0:T(4,128)(2,1)S(1)}, u32[]{:S(2)}, u32[]{:S(2)}) collective-permute-start(bf16[14,3,256]{2,1,0:T(4,128)(2,1)S(1)} %get-tuple-element.47), channel_id=1, source_target_pairs={{0,4},{4,8},{8,12},{12,16},{16,20},{20,24},{24,28},{28,32},{32,36}... | collective-permute-start | bytes 64520 | tf_op jit(solution)/shard_map/ppermute | solution.py:16
  17.5 1.9 collective-permute-start.1
  19.7 3.0 %collective-permute-done.1 = bf16[14,3,256]{2,1,0:T(4,128)(2,1)S(1)} collective-permute-done((bf16[14,3,256]{2,1,0:T(4,128)(2,1)S(1)}, bf16[14,3,256]{2,1,0:T(4,128)(2,1)S(1)}, u32[]{:S(2)}, u32[]{:S(2)}) %collective-permute-start.1) | collective-permute-done | bytes 21536 | tf_op jit(solution)/shard_map/ppermute | solution.py:18
  23.9 2.6 %collective-permute-done.3 = f32[144,128]{1,0:T(8,128)S(1)} collective-permute-done((f32[144,128]{1,0:T(8,128)S(1)}, f32[144,128]{1,0:T(8,128)S(1)}, u32[]{:S(2)}, u32[]{:S(2)}) %collective-permute-start.3) | collective-permute-done | bytes 73760 | tf_op jit(solution)/shard_map/ppermute | solution.py:30
  26.5 6.1 %collective-permute-start.4 = (f32[288,128]{1,0:T(8,128)S(1)}, f32[288,128]{1,0:T(8,128)}, u32[]{:S(2)}, u32[]{:S(2)}) collective-permute-start(f32[288,128]{1,0:T(8,128)S(1)} %constant_dynamic-update-slice_fusion.14), channel_id=1, source_target_pairs={{0,32},{4,36},{8,40},{12,44},{16,48},{20,52},{24,56},{28,60},{32,0... | collective-permute-start | bytes 442376 | tf_op jit(solution)/shard_map/ppermute | solution.py:30
  32.6 2.5 %fusion.62 = (bf16[12,132,256]{2,1,0:T(8,128)(2,1)S(1)}, bf16[12,132,256]{2,1,0:T(8,128)(2,1)S(1)}, bf16[12,132,256]{2,1,0:T(8,128)(2,1)S(1)}, bf16[12,132,256]{...) fusion(bf16[14,134,256]{2,1,0:T(8,128)(2,1)S(1)} %pad_maximum_f, ...), kind=kLoop, calls=%fused_computation.161 | loop fusion | bytes 14598144 | tf_op jit(solution)/shard_map/slice | solution.py:76
  35.1 2.1 reshape.220
  37.2 2.0 reshape.221
  39.2 2.1 reshape.222
  41.3 2.1 reshape.223
  43.4 2.1 reshape.224
  45.4 1.0 reshape.225
  46.4 1.1 reshape.226
  47.7 1.0 reshape.228
  48.7 1.4 fusion.22
  57.9 1.0 reshape.229
  58.9 2.7 %fusion.2 = f32[6,66,256]{2,1,0:T(8,128)S(1)} fusion(f32[6,2,66,2,256]{4,3,2,1,0:T(2,128)S(1)} %reshape.229, f32[256]{0:T(256)S(1)} %copy-done.30), kind=kLoop, calls=%fused_computation.25 | loop fusion | flops 2331648 | bytes 2028544 | tf_op jit(solution)/shard_map/reduce_sum | solution.py:90
  61.6 0.9 constant_dynamic-update-slice_fusion.12
  62.6 2.2 %collective-permute-start.5 = (f32[576,128]{1,0:T(8,128)S(1)}, f32[576,128]{1,0:T(8,128)S(1)}, u32[]{:S(2)}, u32[]{:S(2)}) collective-permute-start(f32[576,128]{1,0:T(8,128)S(1)} %constant_dynamic-update-slice_fusion.12), channel_id=1, source_target_pairs={{0,16},{4,20},{8,24},{12,28},{16,0},{20,4},{24,8},{28,12},{32,48},... | collective-permute-start | bytes 884744 | tf_op jit(solution)/shard_map/ppermute | solution.py:30
  65.0 12.7 %collective-permute-done.5 = f32[576,128]{1,0:T(8,128)S(1)} collective-permute-done((f32[576,128]{1,0:T(8,128)S(1)}, f32[576,128]{1,0:T(8,128)S(1)}, u32[]{:S(2)}, u32[]{:S(2)}) %collective-permute-start.5) | collective-permute-done | bytes 294944 | tf_op jit(solution)/shard_map/ppermute | solution.py:30
  78.8 1.0 stack.2
  79.7 4.2 %all-to-all-start = ((bf16[4,6,66,256]{3,2,1,0:T(8,128)(2,1)}), bf16[4,6,66,256]{3,2,1,0:T(8,128)(2,1)S(1)}, u32[]{:S(2)}, u32[]{:S(2)}) async-start(bf16[4,6,66,256]{3,2,1,0:T(8,128)(2,1)} %stack.2), calls=%async_computation | async-start | bytes 1769472 | tf_op jit(solution)/shard_map/all_to_all | solution.py:136
  83.9 1.1 broadcast_in_dim.64
  85.9 5.0 %collective-permute-done.6 = f32[1152,128]{1,0:T(8,128)S(1)} collective-permute-done((f32[1152,128]{1,0:T(8,128)S(1)}, f32[1152,128]{1,0:T(8,128)S(1)}, u32[]{:S(2)}, u32[]{:S(2)}) %collective-permute-start.6) | collective-permute-done | bytes 589856 | tf_op jit(solution)/shard_map/ppermute | solution.py:30
  90.9 0.9 constant_dynamic-update-slice_fusion.8
  91.7 2.7 %collective-permute-start.7 = (f32[2304,128]{1,0:T(8,128)}, f32[2304,128]{1,0:T(8,128)}, u32[]{:S(2)}, u32[]{:S(2)}) collective-permute-start(f32[2304,128]{1,0:T(8,128)} %constant_dynamic-update-slice_fusion.8), channel_id=1, source_target_pairs={{0,4},{4,0},{8,12},{12,8},{16,20},{20,16},{24,28},{28,24},{32,36},... | collective-permute-start | bytes 3538952 | tf_op jit(solution)/shard_map/ppermute | solution.py:30
  94.6 1.4 constant_dynamic-update-slice_fusion.7
  96.0 1.7 pad_slice_fusion
  101.9 1.4 constant_dynamic-update-slice_fusion.6
  103.5 1.6 slice.251
  105.6 2.2 %gather_fusion.1 = f32[32,128]{1,0:T(8,128)S(1)} fusion(f32[4096,128]{1,0:T(8,128)} %bitcast.146, s32[1024]{0:T(1024)S(1)} %pad_clamp_fusion), kind=kCustom, calls=%fused_computation.1 | custom fusion | bytes 32896 | tf_op jit(solution)/shard_map/gather | solution.py:146
  114.3 2.3 %collective-permute-start.8 = (f32[1184,128]{1,0:T(8,128)S(1)}, f32[1184,128]{1,0:T(8,128)}, u32[]{:S(2)}, u32[]{:S(2)}) collective-permute-start(f32[1184,128]{1,0:T(8,128)S(1)} %constant_dynamic-slice_fusion.5), channel_id=1, source_target_pairs={{0,4},{4,0},{8,12},{12,8},{16,20},{20,16},{24,28},{28,24},{32,36},... | collective-permute-start | bytes 1818632 | tf_op jit(solution)/shard_map/ppermute | solution.py:55
  116.7 1.8 collective-permute-done.8
  118.4 1.1 dynamic-slice_add_fusion
  119.6 1.4 collective-permute-start.9
  121.0 7.1 %collective-permute-done.9 = f32[592,128]{1,0:T(8,128)S(1)} collective-permute-done((f32[592,128]{1,0:T(8,128)S(1)}, f32[592,128]{1,0:T(8,128)S(1)}, u32[]{:S(2)}, u32[]{:S(2)}) %collective-permute-start.9) | collective-permute-done | bytes 303136 | tf_op jit(solution)/shard_map/ppermute | solution.py:55
  128.2 3.4 %collective-permute-start.10 = (f32[296,128]{1,0:T(8,128)S(1)}, f32[296,128]{1,0:T(8,128)S(1)}, u32[]{:S(2)}, u32[]{:S(2)}) collective-permute-start(f32[296,128]{1,0:T(8,128)S(1)} %constant_dynamic-slice_fusion.3), channel_id=1, source_target_pairs={{0,16},{4,20},{8,24},{12,28},{16,0},{20,4},{24,8},{28,12},{32,48},... | collective-permute-start | bytes 454664 | tf_op jit(solution)/shard_map/ppermute | solution.py:55
  131.6 7.4 %collective-permute-done.10 = f32[296,128]{1,0:T(8,128)S(1)} collective-permute-done((f32[296,128]{1,0:T(8,128)S(1)}, f32[296,128]{1,0:T(8,128)S(1)}, u32[]{:S(2)}, u32[]{:S(2)}) %collective-permute-start.10) | collective-permute-done | bytes 151584 | tf_op jit(solution)/shard_map/ppermute | solution.py:55
  139.0 1.7 collective-permute-start.11
  140.7 6.3 %collective-permute-done.11 = f32[148,128]{1,0:T(8,128)S(1)} collective-permute-done((f32[148,128]{1,0:T(8,128)S(1)}, f32[148,128]{1,0:T(8,128)S(1)}, u32[]{:S(2)}, u32[]{:S(2)}) %collective-permute-start.11) | collective-permute-done | bytes 75808 | tf_op jit(solution)/shard_map/ppermute | solution.py:55
  147.1 2.8 %collective-permute-done.12 = f32[74,128]{1,0:T(8,128)S(1)} collective-permute-done((f32[74,128]{1,0:T(8,128)S(1)}, f32[74,128]{1,0:T(8,128)S(1)}, u32[]{:S(2)}, u32[]{:S(2)}) %collective-permute-start.12) | collective-permute-done | bytes 37920 | tf_op jit(solution)/shard_map/ppermute | solution.py:55
  150.8 3.4 %collective-permute-done.13 = f32[37,128]{1,0:T(8,128)S(1)} collective-permute-done((f32[37,128]{1,0:T(8,128)S(1)}, f32[37,128]{1,0:T(8,128)S(1)}, u32[]{:S(2)}, u32[]{:S(2)}) %collective-permute-start.13) | collective-permute-done | bytes 18976 | tf_op jit(solution)/shard_map/ppermute | solution.py:55
  155.1 3.5 %collective-permute-done.14 = f32[69,128]{1,0:T(8,128)S(1)} collective-permute-done((f32[69,128]{1,0:T(8,128)S(1)}, f32[69,128]{1,0:T(8,128)S(1)}, u32[]{:S(2)}, u32[]{:S(2)}) %collective-permute-start.14) | collective-permute-done | bytes 35360 | tf_op jit(solution)/shard_map/ppermute | solution.py:30
  159.6 2.8 %collective-permute-done.15 = f32[138,128]{1,0:T(8,128)S(1)} collective-permute-done((f32[138,128]{1,0:T(8,128)S(1)}, f32[138,128]{1,0:T(8,128)S(1)}, u32[]{:S(2)}, u32[]{:S(2)}) %collective-permute-start.15) | collective-permute-done | bytes 70688 | tf_op jit(solution)/shard_map/ppermute | solution.py:30
  162.8 1.9 collective-permute-start.16
  164.7 1.1 dynamic_update_slice.88
  165.8 4.9 %collective-permute-done.16 = f32[276,128]{1,0:T(8,128)S(1)} collective-permute-done((f32[276,128]{1,0:T(8,128)S(1)}, f32[276,128]{1,0:T(8,128)S(1)}, u32[]{:S(2)}, u32[]{:S(2)}) %collective-permute-start.16) | collective-permute-done | bytes 141344 | tf_op jit(solution)/shard_map/ppermute | solution.py:30
  171.6 11.0 %collective-permute-done.17 = f32[552,128]{1,0:T(8,128)S(1)} collective-permute-done((f32[552,128]{1,0:T(8,128)S(1)}, f32[552,128]{1,0:T(8,128)S(1)}, u32[]{:S(2)}, u32[]{:S(2)}) %collective-permute-start.17) | collective-permute-done | bytes 282656 | tf_op jit(solution)/shard_map/ppermute | solution.py:30
  182.9 12.0 %collective-permute-done.18 = f32[1104,128]{1,0:T(8,128)S(1)} collective-permute-done((f32[1104,128]{1,0:T(8,128)S(1)}, f32[1104,128]{1,0:T(8,128)S(1)}, u32[]{:S(2)}, u32[]{:S(2)}) %collective-permute-start.18) | collective-permute-done | bytes 565280 | tf_op jit(solution)/shard_map/ppermute | solution.py:30
  194.9 6.0 %collective-permute-start.19 = (f32[2208,128]{1,0:T(8,128)S(1)}, f32[2208,128]{1,0:T(8,128)S(1)}, u32[]{:S(2)}, u32[]{:S(2)}) collective-permute-start(f32[2208,128]{1,0:T(8,128)S(1)} %constant_dynamic-update-slice_fusion.2), channel_id=1, source_target_pairs={{0,4},{4,0},{8,12},{12,8},{16,20},{20,16},{24,28},{28,24},{32,36},... | collective-permute-start | bytes 3391496 | tf_op jit(solution)/shard_map/ppermute | solution.py:30
  201.3 1.5 broadcast_in_dim.71
  202.8 1.1 constant_dynamic-update-slice_fusion.1
  203.9 1.1 constant_dynamic-update-slice_fusion
  205.0 1.7 reshape.243
  206.7 1.2 slice.257
  207.9 2.4 %reshape.245 = f32[2368,128]{1,0:T(8,128)} reshape(f32[64,37,128]{2,1,0:T(8,128)} %slice.257) | data formatting | bytes 2424832 | tf_op jit(solution)/shard_map/reshape | solution.py:59
  210.3 2.4 %slice.258 = f32[2304,128]{1,0:T(8,128)} slice(f32[2368,128]{1,0:T(8,128)} %reshape.245), slice={[0:2304], [0:128]} | slice | bytes 2359296 | tf_op jit(solution)/shard_map/slice | solution.py:176
  212.6 1.2 slice_bitcast_fusion
  214.0 1.2 convolution_divide_fusion
  (171 shorter events, 29.8 us)
Async XLA Ops:
  8.5 14.6 %collective-permute-start.2 = (f32[72,128]{1,0:T(8,128)S(1)}, f32[72,128]{1,0:T(8,128)S(1)}, u32[]{:S(2)}, u32[]{:S(2)}) collective-permute-start(f32[72,128]{1,0:T(8,128)S(1)} %get-tuple-element.67), channel_id=1, source_target_pairs={{0,128},{4,132},{8,136},{12,140},{16,144},{20,148},{24,152},{28,15... | collective-permute-start | bytes 110600 | tf_op jit(solution)/shard_map/ppermute | solution.py:30
  12.1 7.4 %copy-start.1 = (bf16[48,128,256]{2,1,0:T(8,128)(2,1)S(1)}, bf16[48,128,256]{2,1,0:T(8,128)(2,1)}, u32[]{:S(2)}) copy-start(bf16[48,128,256]{2,1,0:T(8,128)(2,1)} %param.15) | copy-start | bytes 9437188
  13.1 6.6 %collective-permute-start = (bf16[14,3,256]{2,1,0:T(4,128)(2,1)S(1)}, bf16[14,3,256]{2,1,0:T(4,128)(2,1)S(1)}, u32[]{:S(2)}, u32[]{:S(2)}) collective-permute-start(bf16[14,3,256]{2,1,0:T(4,128)(2,1)S(1)} %get-tuple-element.47), channel_id=1, source_target_pairs={{0,4},{4,8},{8,12},{12,16},{16,20},{20,24},{24,28},{28,32},{32,36}... | collective-permute-start | bytes 64520 | tf_op jit(solution)/shard_map/ppermute | solution.py:16
  17.5 2.1 copy-start.31
  17.5 5.2 %collective-permute-start.1 = (bf16[14,3,256]{2,1,0:T(4,128)(2,1)S(1)}, bf16[14,3,256]{2,1,0:T(4,128)(2,1)S(1)}, u32[]{:S(2)}, u32[]{:S(2)}) collective-permute-start(bf16[14,3,256]{2,1,0:T(4,128)(2,1)S(1)} %get-tuple-element.48), channel_id=1, source_target_pairs={{4,0},{8,4},{12,8},{16,12},{20,16},{24,20},{28,24},{32,28},{36,32}... | collective-permute-start | bytes 64520 | tf_op jit(solution)/shard_map/ppermute | solution.py:18
  23.2 3.3 %collective-permute-start.3 = (f32[144,128]{1,0:T(8,128)S(1)}, f32[144,128]{1,0:T(8,128)S(1)}, u32[]{:S(2)}, u32[]{:S(2)}) collective-permute-start(f32[144,128]{1,0:T(8,128)S(1)} %constant_dynamic-update-slice_fusion.16), channel_id=1, source_target_pairs={{0,64},{4,68},{8,72},{12,76},{16,80},{20,84},{24,88},{28,92},{32,9... | collective-permute-start | bytes 221192 | tf_op jit(solution)/shard_map/ppermute | solution.py:30
  26.5 35.2 %collective-permute-start.4 = (f32[288,128]{1,0:T(8,128)S(1)}, f32[288,128]{1,0:T(8,128)}, u32[]{:S(2)}, u32[]{:S(2)}) collective-permute-start(f32[288,128]{1,0:T(8,128)S(1)} %constant_dynamic-update-slice_fusion.14), channel_id=1, source_target_pairs={{0,32},{4,36},{8,40},{12,44},{16,48},{20,52},{24,56},{28,60},{32,0... | collective-permute-start | bytes 442376 | tf_op jit(solution)/shard_map/ppermute | solution.py:30
  47.5 1.2 copy-start.20
  48.7 1.4 copy-start.27
  48.7 1.6 copy-start.28
  50.3 1.1 copy-start.26
  51.4 1.1 copy-start.25
  52.6 1.1 copy-start.24
  53.7 1.1 copy-start.23
  54.8 1.1 copy-start.22
  56.4 1.1 copy-start.21
  57.9 1.0 copy-start.30
  62.6 15.5 %copy-start = (s32[64]{0:T(128)S(1)}, s32[64]{0:T(128)}, u32[]{:S(2)}) copy-start(s32[64]{0:T(128)} %constant.336.clone) | copy-start | bytes 772
  62.6 15.1 %collective-permute-start.5 = (f32[576,128]{1,0:T(8,128)S(1)}, f32[576,128]{1,0:T(8,128)S(1)}, u32[]{:S(2)}, u32[]{:S(2)}) collective-permute-start(f32[576,128]{1,0:T(8,128)S(1)} %constant_dynamic-update-slice_fusion.12), channel_id=1, source_target_pairs={{0,16},{4,20},{8,24},{12,28},{16,0},{20,4},{24,8},{28,12},{32,48},... | collective-permute-start | bytes 884744 | tf_op jit(solution)/shard_map/ppermute | solution.py:30
  77.7 13.1 %collective-permute-start.6 = (f32[1152,128]{1,0:T(8,128)S(1)}, f32[1152,128]{1,0:T(8,128)S(1)}, u32[]{:S(2)}, u32[]{:S(2)}) collective-permute-start(f32[1152,128]{1,0:T(8,128)S(1)} %constant_dynamic-update-slice_fusion.10), channel_id=1, source_target_pairs={{0,8},{4,12},{8,0},{12,4},{16,24},{20,28},{24,16},{28,20},{32,40},... | collective-permute-start | bytes 1769480 | tf_op jit(solution)/shard_map/ppermute | solution.py:30
  79.7 16.2 %all-to-all-start = ((bf16[4,6,66,256]{3,2,1,0:T(8,128)(2,1)}), bf16[4,6,66,256]{3,2,1,0:T(8,128)(2,1)S(1)}, u32[]{:S(2)}, u32[]{:S(2)}) async-start(bf16[4,6,66,256]{3,2,1,0:T(8,128)(2,1)} %stack.2), calls=%async_computation | async-start | bytes 1769472 | tf_op jit(solution)/shard_map/all_to_all | solution.py:136
  91.7 10.2 %collective-permute-start.7 = (f32[2304,128]{1,0:T(8,128)}, f32[2304,128]{1,0:T(8,128)}, u32[]{:S(2)}, u32[]{:S(2)}) collective-permute-start(f32[2304,128]{1,0:T(8,128)} %constant_dynamic-update-slice_fusion.8), channel_id=1, source_target_pairs={{0,4},{4,0},{8,12},{12,8},{16,20},{20,16},{24,28},{28,24},{32,36},... | collective-permute-start | bytes 3538952 | tf_op jit(solution)/shard_map/ppermute | solution.py:30
  95.9 1.8 copy-start.29
  97.6 1.2 copy-start.12
  97.7 1.6 copy-start.14
  97.7 1.6 copy-start.16
  97.7 1.8 copy-start.18
  97.7 2.1 copy-start.10
  97.7 2.4 %copy-start.8 = (bf16[24,64,256]{2,1,0:T(8,128)(2,1)}, bf16[24,64,256]{2,1,0:T(8,128)(2,1)S(1)}, u32[]{:S(2)}) copy-start(bf16[24,64,256]{2,1,0:T(8,128)(2,1)S(1)} %get-tuple-element.63) | copy-start | bytes 2359300
  97.7 2.8 %copy-start.6 = (bf16[24,64,256]{2,1,0:T(8,128)(2,1)}, bf16[24,64,256]{2,1,0:T(8,128)(2,1)S(1)}, u32[]{:S(2)}) copy-start(bf16[24,64,256]{2,1,0:T(8,128)(2,1)S(1)} %get-tuple-element.61) | copy-start | bytes 2359300
  97.7 3.2 %copy-start.4 = (bf16[24,64,256]{2,1,0:T(8,128)(2,1)}, bf16[24,64,256]{2,1,0:T(8,128)(2,1)S(1)}, u32[]{:S(2)}) copy-start(bf16[24,64,256]{2,1,0:T(8,128)(2,1)S(1)} %get-tuple-element.62) | copy-start | bytes 2359300
  97.7 3.5 %copy-start.2 = (bf16[24,64,256]{2,1,0:T(8,128)(2,1)}, bf16[24,64,256]{2,1,0:T(8,128)(2,1)S(1)}, u32[]{:S(2)}) copy-start(bf16[24,64,256]{2,1,0:T(8,128)(2,1)S(1)} %get-tuple-element.58) | copy-start | bytes 2359300
  100.9 0.7 copy-start.32
  107.8 1.1 copy-start.19
  108.6 1.2 copy-start.17
  108.9 1.3 copy-start.15
  109.8 1.2 copy-start.13
  110.3 1.2 copy-start.11
  111.0 1.2 copy-start.9
  111.5 1.2 copy-start.7
  112.2 1.2 copy-start.5
  112.7 1.2 copy-start.3
  114.3 4.1 %collective-permute-start.8 = (f32[1184,128]{1,0:T(8,128)S(1)}, f32[1184,128]{1,0:T(8,128)}, u32[]{:S(2)}, u32[]{:S(2)}) collective-permute-start(f32[1184,128]{1,0:T(8,128)S(1)} %constant_dynamic-slice_fusion.5), channel_id=1, source_target_pairs={{0,4},{4,0},{8,12},{12,8},{16,20},{20,16},{24,28},{28,24},{32,36},... | collective-permute-start | bytes 1818632 | tf_op jit(solution)/shard_map/ppermute | solution.py:55
  119.6 8.5 %collective-permute-start.9 = (f32[592,128]{1,0:T(8,128)S(1)}, f32[592,128]{1,0:T(8,128)S(1)}, u32[]{:S(2)}, u32[]{:S(2)}) collective-permute-start(f32[592,128]{1,0:T(8,128)S(1)} %constant_dynamic-slice_fusion.4), channel_id=1, source_target_pairs={{0,8},{4,12},{8,0},{12,4},{16,24},{20,28},{24,16},{28,20},{32,40},... | collective-permute-start | bytes 909320 | tf_op jit(solution)/shard_map/ppermute | solution.py:55
  128.2 10.8 %collective-permute-start.10 = (f32[296,128]{1,0:T(8,128)S(1)}, f32[296,128]{1,0:T(8,128)S(1)}, u32[]{:S(2)}, u32[]{:S(2)}) collective-permute-start(f32[296,128]{1,0:T(8,128)S(1)} %constant_dynamic-slice_fusion.3), channel_id=1, source_target_pairs={{0,16},{4,20},{8,24},{12,28},{16,0},{20,4},{24,8},{28,12},{32,48},... | collective-permute-start | bytes 454664 | tf_op jit(solution)/shard_map/ppermute | solution.py:55
  139.0 7.9 %collective-permute-start.11 = (f32[148,128]{1,0:T(8,128)S(1)}, f32[148,128]{1,0:T(8,128)S(1)}, u32[]{:S(2)}, u32[]{:S(2)}) collective-permute-start(f32[148,128]{1,0:T(8,128)S(1)} %constant_dynamic-slice_fusion.2), channel_id=1, source_target_pairs={{0,32},{4,36},{8,40},{12,44},{16,48},{20,52},{24,56},{28,60},{32,0... | collective-permute-start | bytes 227336 | tf_op jit(solution)/shard_map/ppermute | solution.py:55
  147.0 2.9 %collective-permute-start.12 = (f32[74,128]{1,0:T(8,128)S(1)}, f32[74,128]{1,0:T(8,128)S(1)}, u32[]{:S(2)}, u32[]{:S(2)}) collective-permute-start(f32[74,128]{1,0:T(8,128)S(1)} %constant_dynamic-slice_fusion.1), channel_id=1, source_target_pairs={{0,64},{4,68},{8,72},{12,76},{16,80},{20,84},{24,88},{28,92},{32,9... | collective-permute-start | bytes 113672 | tf_op jit(solution)/shard_map/ppermute | solution.py:55
  150.0 4.2 %collective-permute-start.13 = (f32[37,128]{1,0:T(8,128)S(1)}, f32[37,128]{1,0:T(8,128)S(1)}, u32[]{:S(2)}, u32[]{:S(2)}) collective-permute-start(f32[37,128]{1,0:T(8,128)S(1)} %constant_dynamic-slice_fusion), channel_id=1, source_target_pairs={{0,128},{4,132},{8,136},{12,140},{16,144},{20,148},{24,152},{28,15... | collective-permute-start | bytes 56840 | tf_op jit(solution)/shard_map/ppermute | solution.py:55
  154.2 4.4 %collective-permute-start.14 = (f32[69,128]{1,0:T(8,128)S(1)}, f32[69,128]{1,0:T(8,128)S(1)}, u32[]{:S(2)}, u32[]{:S(2)}) collective-permute-start(f32[69,128]{1,0:T(8,128)S(1)} %pad_maximum_fusion.2), channel_id=1, source_target_pairs={{0,128},{4,132},{8,136},{12,140},{16,144},{20,148},{24,152},{28,15... | collective-permute-start | bytes 105992 | tf_op jit(solution)/shard_map/ppermute | solution.py:30
  158.9 3.6 %collective-permute-start.15 = (f32[138,128]{1,0:T(8,128)S(1)}, f32[138,128]{1,0:T(8,128)S(1)}, u32[]{:S(2)}, u32[]{:S(2)}) collective-permute-start(f32[138,128]{1,0:T(8,128)S(1)} %dynamic_update_slice.85), channel_id=1, source_target_pairs={{0,64},{4,68},{8,72},{12,76},{16,80},{20,84},{24,88},{28,92},{32,9... | collective-permute-start | bytes 211976 | tf_op jit(solution)/shard_map/ppermute | solution.py:30
  162.8 7.9 %collective-permute-start.16 = (f32[276,128]{1,0:T(8,128)S(1)}, f32[276,128]{1,0:T(8,128)S(1)}, u32[]{:S(2)}, u32[]{:S(2)}) collective-permute-start(f32[276,128]{1,0:T(8,128)S(1)} %dynamic_update_slice.87), channel_id=1, source_target_pairs={{0,32},{4,36},{8,40},{12,44},{16,48},{20,52},{24,56},{28,60},{32,0... | collective-permute-start | bytes 423944 | tf_op jit(solution)/shard_map/ppermute | solution.py:30
  171.4 11.2 %collective-permute-start.17 = (f32[552,128]{1,0:T(8,128)S(1)}, f32[552,128]{1,0:T(8,128)S(1)}, u32[]{:S(2)}, u32[]{:S(2)}) collective-permute-start(f32[552,128]{1,0:T(8,128)S(1)} %dynamic_update_slice.89), channel_id=1, source_target_pairs={{0,16},{4,20},{8,24},{12,28},{16,0},{20,4},{24,8},{28,12},{32,48},... | collective-permute-start | bytes 847880 | tf_op jit(solution)/shard_map/ppermute | solution.py:30
  182.7 12.2 %collective-permute-start.18 = (f32[1104,128]{1,0:T(8,128)S(1)}, f32[1104,128]{1,0:T(8,128)S(1)}, u32[]{:S(2)}, u32[]{:S(2)}) collective-permute-start(f32[1104,128]{1,0:T(8,128)S(1)} %constant_dynamic-update-slice_fusion.4), channel_id=1, source_target_pairs={{0,8},{4,12},{8,0},{12,4},{16,24},{20,28},{24,16},{28,20},{32,40},... | collective-permute-start | bytes 1695752 | tf_op jit(solution)/shard_map/ppermute | solution.py:30
  194.9 9.0 %collective-permute-start.19 = (f32[2208,128]{1,0:T(8,128)S(1)}, f32[2208,128]{1,0:T(8,128)S(1)}, u32[]{:S(2)}, u32[]{:S(2)}) collective-permute-start(f32[2208,128]{1,0:T(8,128)S(1)} %constant_dynamic-update-slice_fusion.2), channel_id=1, source_target_pairs={{0,4},{4,0},{8,12},{12,8},{16,20},{20,16},{24,28},{28,24},{32,36},... | collective-permute-start | bytes 3391496 | tf_op jit(solution)/shard_map/ppermute | solution.py:30
